TPU v7x, 32 devices: a whole 2x2x4 slice. The times are simulated.
32 devices in a mesh: slab: 8 (over z, core), loop: 4 (over y, x).
Axes of the slice: x: 2, y: 2, z: 4, core: 2. Of those that a mesh axis runs over, the one named last changes fastest.
Arguments:
- doc_pool: bfloat16 [8, 4, 256, 4096], P('slab', 'loop'), may hold values from -6 to 6
- cand_owner: int32 [8, 4, 16, 1], P('slab', 'loop'), may hold values from 0 to 7; in each aligned block of 16 rows (0 to 15, 16 to 31, ..., all dimensions but the last counted through in order) at most 4 rows name the same one
- cand_row: int32 [8, 4, 16], P('slab', 'loop'), may hold values from 0 to 255
- elements: bfloat16 [8, 4, 2048, 4096], P('slab', 'loop'), may hold values from -6 to 6
- coverage: float32 [8, 4, 2048], P('slab', 'loop'), may hold values from -0.5 to 1.5
- elem_weight: float32 [8, 4, 2048], P('slab', 'loop'), may hold values from 1 to 10
Outputs:
- gains: float32 [8, 4, 16], P('slab', 'loop')
Inputs may be any that keep to these rules, and one draw needn't show every extreme that they name: `cand_owner`: among the candidates of one device, at most 4 name the same owner; some owner is named exactly 4 times.
All inputs are finite; a program needn't handle non-finite values.
Results may differ from a plain program's by a relative error of at most 0.0003.
Values may be sent and summed in bfloat16 or wider, within the bound.
A program may use at most 128 MiB of HBM per device.

v0:
```python
import jax
import jax.numpy as jnp
from jax import lax
from jax.sharding import PartitionSpec as P


def body(doc_pool, cand_owner, cand_row, elements, coverage, elem_weight):
    slab_count = lax.axis_size("slab")
    loop_count = lax.axis_size("loop")
    share_len = cand_row.shape[2]
    width = doc_pool.shape[3]
    slot_cap = max(2, 2 * share_len // slab_count)
    pool_local = doc_pool.reshape(doc_pool.shape[2], width)
    owner_ids = cand_owner.reshape(share_len)
    row_ids = cand_row.reshape(share_len)
    docs = elements.reshape(elements.shape[2], width)
    cover_local = coverage.reshape(coverage.shape[2])
    weight_local = elem_weight.reshape(elem_weight.shape[2])
    sim_scale = float(width) ** (-0.5)
    element_total = float(docs.shape[0] * slab_count * loop_count)
    positions = jnp.arange(share_len, dtype=jnp.int32)
    same_owner = owner_ids[:, None] == owner_ids[None, :]
    earlier = positions[None, :] < positions[:, None]
    slot_rank = jnp.sum((same_owner & earlier).astype(jnp.int32), axis=1)
    slot_id = owner_ids * slot_cap + slot_rank
    onehot = (
        slot_id[:, None] == jnp.arange(slab_count * slot_cap, dtype=jnp.int32)[None, :]
    ).astype(jnp.int32)
    requests = jnp.sum(onehot * row_ids[:, None], axis=0).reshape(slab_count, slot_cap)
    doc_rows = jnp.take(
        pool_local,
        lax.all_to_all(requests, "slab", split_axis=0, concat_axis=0, tiled=True),
        axis=0,
    )
    fetched = lax.all_to_all(doc_rows, "slab", split_axis=0, concat_axis=0, tiled=True)
    cand_rows = jnp.take(fetched.reshape(slab_count * slot_cap, width), slot_id, axis=0)
    scores = (
        lax.dot_general(
            docs,
            lax.all_gather(cand_rows, ("slab", "loop"), axis=0, tiled=True),
            (((1,), (1,)), ((), ())),
            preferred_element_type=jnp.float32,
        )
        * sim_scale
    )
    running = (
        jnp.sum(weight_local[:, None] * jnp.maximum(scores - cover_local[:, None], 0.0), axis=0)
        / element_total
    )
    terms = running.reshape(slab_count * loop_count, share_len)
    summed = lax.psum_scatter(terms, ("slab", "loop"), scatter_dimension=0, tiled=True)
    return summed.reshape(1, 1, share_len)


def solution(mesh):
    placed = (
        P("slab", "loop", None, None),
        P("slab", "loop", None, None),
        P("slab", "loop", None),
        P("slab", "loop", None, None),
        P("slab", "loop", None),
        P("slab", "loop", None),
    )
    return jax.shard_map(
        body, mesh=mesh, in_specs=placed, out_specs=P("slab", "loop", None), check_vma=False
    )
```

profile of v0, /device:TPU:0, one launch (start us, length us, event | category | flops | bytes accessed | tf_op | source)
XLA Modules:
  0.0 158.7 jit_solution(5198425859005302482)
XLA Ops:
  6.5 1.0 convert_reduce_fusion
  7.5 0.7 compare_and_fusion.1
  8.2 0.7 select_reduce_fusion
  9.0 0.1 all_to_all.13
  9.0 11.7 %all_to_all.20 = s32[8,1,4]{2,1,0:T(1,128)S(1)} all-to-all(s32[8,1,4]{2,1,0:T(1,128)S(1)} %bitcast.33), channel_id=1, replica_groups=mesh['slab'=8,'loop'=4] {'slab'}, dimensions={0} | all-to-all | bytes 256 | tf_op jit(solution)/shard_map/all_to_all | solution.py:32
  20.8 0.1 copy.21
  20.9 0.1 copy.24
  20.9 0.1 reshape.109
  21.0 0.7 gather_fusion
  21.8 0.1 reshape.108
  21.9 0.1 copy.22
  22.0 0.9 broadcast_select_fusion
  22.8 3.4 %all-to-all-start.1 = ((bf16[8,4,4096]{2,1,0:T(4,128)(2,1)}), bf16[8,4,4096]{2,1,0:T(4,128)(2,1)S(1)}, u32[]{:S(2)}, u32[]{:S(2)}) async-start(bf16[8,4,4096]{2,1,0:T(4,128)(2,1)} %broadcast_select_fusion), calls=%async_computation.1 | async-start | bytes 524288 | tf_op jit(solution)/shard_map/all_to_all | solution.py:35
  26.3 0.0 all-gather.2.cloned.1.call-start
  26.3 0.7 fusion.5
  27.0 8.9 %all-to-all-done.1 = bf16[8,4,4096]{2,1,0:T(4,128)(2,1)S(1)} async-done(((bf16[8,4,4096]{2,1,0:T(4,128)(2,1)}), bf16[8,4,4096]{2,1,0:T(4,128)(2,1)S(1)}, u32[]{:S(2)}, u32[]{:S(2)}) %all-to-all-start.1) | async-done | bytes 262176 | tf_op jit(solution)/shard_map/all_to_all | solution.py:35
  35.9 0.1 reshape.104
  36.0 0.6 gather_fusion.1
  36.6 0.7 broadcast_select_fusion.1
  37.3 60.8 %all-gather.2.cloned.1.call-done = bf16[512,4096]{1,0:T(8,128)(2,1)} async-done(((bf16[16,4096]{1,0:T(8,128)(2,1)}), bf16[512,4096]{1,0:T(8,128)(2,1)}) %all-gather.2.cloned.1.call-update) | async-done | bytes 4194320 | tf_op jit(solution)/shard_map/all_gather | solution.py:40
  98.1 14.0 %multiply_reduce_fusion = f32[512]{0:T(512)S(1)} fusion(bf16[512,4096]{1,0:T(8,128)(2,1)} %all-gather.2.cloned.1.call-done, bf16[1,1,2048,4096]{3,2,1,0:T(8,128)(2,1)} %param.9, f32[2048]{0:T(1024)S(1)} %bitcast.35, f32[2048]{0:T(1024)S(1)} %bitcast.36), kind=kOutput, calls=%fused_computation.4 | convolution fusion | flops 8595177472 | bytes 20989952 | tf_op jit(solution)/shard_map/dot_general | solution.py:38
  112.1 0.1 div.10
  112.2 39.2 %all-reduce = f32[32,16]{1,0:T(8,128)S(1)} all-reduce(f32[32,16]{1,0:T(8,128)S(1)} %div.10), channel_id=2, replica_groups=mesh['slab'=8,'loop'=4] {'slab','loop'}, use_global_device_ids=true, to_apply=%region_3.4.clone | all-reduce | flops 512 | bytes 4096
  151.3 0.5 dynamic-slice_bitcast_fusion
  (12 shorter events, 0.1 us)
Async XLA Ops:
  6.5 14.5 %copy-start = (bf16[1,1,256,4096]{3,2,1,0:T(8,128)(2,1)S(1)}, bf16[1,1,256,4096]{3,2,1,0:T(8,128)(2,1)}, u32[]{:S(2)}) copy-start(bf16[1,1,256,4096]{3,2,1,0:T(8,128)(2,1)} %param.6) | copy-start | bytes 6291460
  6.5 91.6 %copy-start.2 = (f32[1,1,2048]{2,1,0:T(1,128)S(1)}, f32[1,1,2048]{2,1,0:T(1,128)}, u32[]{:S(2)}) copy-start(f32[1,1,2048]{2,1,0:T(1,128)} %param.11) | copy-start | bytes 24580
  6.5 91.6 %copy-start.1 = (f32[1,1,2048]{2,1,0:T(1,128)S(1)}, f32[1,1,2048]{2,1,0:T(1,128)}, u32[]{:S(2)}) copy-start(f32[1,1,2048]{2,1,0:T(1,128)} %param.10) | copy-start | bytes 24580
  22.8 13.1 %all-to-all-start.1 = ((bf16[8,4,4096]{2,1,0:T(4,128)(2,1)}), bf16[8,4,4096]{2,1,0:T(4,128)(2,1)S(1)}, u32[]{:S(2)}, u32[]{:S(2)}) async-start(bf16[8,4,4096]{2,1,0:T(4,128)(2,1)} %broadcast_select_fusion), calls=%async_computation.1 | async-start | bytes 524288 | tf_op jit(solution)/shard_map/all_to_all | solution.py:35
  26.3 71.8 %all-gather.2.cloned.1.call-start = ((), (), s32[]{:S(2)}) async-start(), calls=%async_computation.2 | async-start | bytes 4325376 | tf_op jit(solution)/shard_map/all_gather | solution.py:40
Sparse Core Ops, SparseCore 0:
  37.5 60.5 all-gather.1
where the time goes:
time: 159 us
  waiting for transfers between devices  69.7 us (44%)
  blocking collectives  50.9 us (32%)
  matrix products  14 us (9%)
  between operations  13.5 us (8%)
  other arithmetic  4.71 us (3%)
  starting transfers between devices  3.45 us (2%)
  local copies, waits for them, and re-layouts  2.52 us (2%)
    all_gather x1, waiting for transfers between devices, body(): lax.all_gather(cand_rows, ('slab', 'loop'), axis=0, tiled=True)  60.8 us
    unnamed x1, blocking collectives  39.2 us
    dot_general x1, matrix products, body(): lax.dot_general(docs, lax.all_gather(cand_rows, ('slab', 'loop'), axis=0,...  14 us
    all_to_all x1, blocking collectives, body(): lax.all_to_all(requests, 'slab', split_axis=0, concat_axis=0, tiled=True)  11.7 us
    all_to_all x1, waiting for transfers between devices, body(): lax.all_to_all(doc_rows, 'slab', split_axis=0, concat_axis=0, tiled=True)  8.91 us
    all_to_all x1, starting transfers between devices, body(): lax.all_to_all(doc_rows, 'slab', split_axis=0, concat_axis=0, tiled=True)  3.41 us
  transfers between devices with their start and end apart: 2, of which 2 were waited for; matrix products, arithmetic and copies ran while one was open for 0% of the time, Pallas kernels for 0%

commit v1 on v0

v1 whole, which is shorter than its diff:
```python
import functools

import jax
import jax.numpy as jnp
from jax import lax
from jax.experimental import pallas as pl
from jax.experimental.pallas import tpu as pltpu
from jax.sharding import PartitionSpec as P

MESH = pl.DeviceIdType.MESH
LANES = 128
SUB = 8


def kernel(
    dims,
    owner_ref, row_ref, cover_ref, weight_ref, pool_hbm, docs_hbm,
    out_ref,
    pool, docs, req_out, req_in, picked, fetched, cand, acc, part, terms,
    pool_sem, docs_sem, req_send, req_recv, pick_send, pick_recv, self_sem,
    unit_send, unit_recv, term_send, term_recv,
):
    slabs, loops, share, cap, chunks, chunk, tile, total_docs, scale = dims
    lines = slabs // 2
    units = slabs * loops
    rows_pool = pool.shape[0]
    n_docs = docs.shape[1]
    slab = lax.axis_index("slab")
    loop = lax.axis_index("loop")
    line = slab // 2
    core = lax.rem(slab, 2)
    me = slab * loops + loop
    half = loops // 2

    def loop_of(pos):
        return jnp.where(pos < half, 2 * pos, 2 * (loops - 1 - pos) + 1)

    here = jnp.where(lax.rem(loop, 2) == 0, loop // 2, loops - 1 - loop // 2)
    ahead = loop_of(lax.rem(here + 1, loops))
    behind = loop_of(lax.rem(here + loops - 1, loops))

    pool_copy = [
        pltpu.make_async_copy(
            pool_hbm.at[:, pl.ds(k * chunk, chunk)],
            pool.at[:, pl.ds(k * chunk, chunk)],
            pool_sem.at[k],
        )
        for k in range(chunks)
    ]
    docs_copy = [
        pltpu.make_async_copy(
            docs_hbm.at[:, pl.ds(k * chunk, chunk)], docs.at[k], docs_sem.at[k]
        )
        for k in range(chunks)
    ]

    barrier = pltpu.get_barrier_semaphore()

    def greet(d, _):
        other = lax.rem(me + d, units)
        pl.semaphore_signal(
            barrier, inc=1, device_id=(other // loops, lax.rem(other, loops)), device_id_type=MESH
        )
        return 0

    lax.fori_loop(1, units, greet, 0)
    for k in range(chunks):
        pool_copy[k].start()
    for k in range(chunks):
        docs_copy[k].start()

    owner_row = owner_ref[...]
    row_row = row_ref[...]
    down = lax.broadcasted_iota(jnp.int32, (share, share), 0)
    across = lax.broadcasted_iota(jnp.int32, (share, share), 1)
    wide = jnp.broadcast_to(owner_row, (share, share)).astype(jnp.float32)
    owner_col = jnp.sum(jnp.where(down == across, wide, 0.0), axis=1, keepdims=True)
    rank_row = jnp.sum(
        jnp.where((owner_col == wide) & (down < across), 1.0, 0.0), axis=0, keepdims=True
    )
    owner_f = owner_row.astype(jnp.float32)
    asked_row = owner_f * SUB + rank_row
    slot_row = owner_f * cap + rank_row
    slot_col = jnp.sum(
        jnp.where(down == across, jnp.broadcast_to(slot_row, (share, share)), 0.0),
        axis=1, keepdims=True,
    )
    place = lax.broadcasted_iota(jnp.int32, (slabs * SUB, share), 0).astype(jnp.float32)
    asked = jnp.sum(
        jnp.where(place == asked_row, row_row.astype(jnp.float32), 0.0), axis=1, keepdims=True
    )
    req_out[...] = jnp.broadcast_to(asked, (slabs * SUB, LANES)).astype(jnp.int32).reshape(
        slabs, SUB, LANES
    )
    choose = jnp.where(
        slot_col == lax.broadcasted_iota(jnp.int32, (share, slabs * cap), 1).astype(jnp.float32),
        1.0, 0.0,
    ).astype(jnp.bfloat16)

    pl.semaphore_wait(barrier, units - 1)

    def req_copy(d):
        other = lax.rem(slab + d, slabs)
        return pltpu.make_async_remote_copy(
            src_ref=req_out.at[other], dst_ref=req_in.at[slab],
            send_sem=req_send.at[d], recv_sem=req_recv.at[d],
            device_id=(other, loop), device_id_type=MESH,
        )

    for d in range(1, slabs):
        req_copy(d).start()
    own_req = pltpu.make_async_copy(req_out.at[slab], req_in.at[slab], self_sem.at[chunks])
    own_req.start()
    own_req.wait()
    for d in range(1, slabs):
        req_copy(d).wait()

    wanted = req_in[...].reshape(slabs * SUB, LANES)
    lane = lax.broadcasted_iota(jnp.int32, (slabs * SUB, LANES), 1)
    pick = jnp.concatenate(
        [
            jnp.where(wanted == lane + b * LANES, 1.0, 0.0).astype(jnp.bfloat16)
            for b in range(rows_pool // LANES)
        ],
        axis=1,
    )

    def pick_copy(k, d):
        other = lax.rem(slab + d, slabs)
        return pltpu.make_async_remote_copy(
            src_ref=picked.at[k, other], dst_ref=fetched.at[k, slab],
            send_sem=pick_send.at[k, d], recv_sem=pick_recv.at[k, d],
            device_id=(other, loop), device_id_type=MESH,
        )

    def own_pick(k):
        return pltpu.make_async_copy(picked.at[k, slab], fetched.at[k, slab], self_sem.at[k])

    def gather(k):
        pool_copy[k].wait()
        rows = jnp.dot(
            pick, pool[:, k * chunk:(k + 1) * chunk], preferred_element_type=jnp.float32
        )
        for r in range(slabs):
            picked[k, r] = rows[r * SUB:r * SUB + cap].astype(jnp.bfloat16)
        for d in range(1, slabs):
            pick_copy(k, d).start()
        own_pick(k).start()

    def unit_of(j, pos, c):
        return (2 * j + c) * loops + loop_of(pos)

    def unit_copy(k, j, pos, way):
        u = unit_of(j, pos, core)
        if way == 0:
            device = (2 * jnp.minimum(line + 1, lines - 1) + core, loop)
        elif way == 1:
            device = (2 * jnp.maximum(line - 1, 0) + core, loop)
        elif way == 2:
            device = (slab, ahead)
        elif way == 3:
            device = (slab, behind)
        else:
            device = (2 * line + 1 - core, loop)
        return pltpu.make_async_remote_copy(
            src_ref=cand.at[k, u], dst_ref=cand.at[k, u],
            send_sem=unit_send.at[k, j * loops + pos, way], recv_sem=unit_recv.at[k, u],
            device_id=device, device_id_type=MESH,
        )

    def arrive(k, j, pos, c):
        u = unit_of(j, pos, c)
        pltpu.make_async_remote_copy(
            src_ref=cand.at[k, u], dst_ref=cand.at[k, u],
            send_sem=unit_send.at[k, 0, 0], recv_sem=unit_recv.at[k, u],
            device_id=(2 * line + 1 - core, loop), device_id_type=MESH,
        ).wait_recv()

    reach_even, reach_odd = half, loops - 1 - half

    def forward(k, j, pos, finish=False):
        def act(cond, way):
            @pl.when(cond)
            def _():
                copy = unit_copy(k, j, pos, way)
                if finish:
                    copy.wait_send()
                else:
                    copy.start()
        from_here = pos == here
        far_ahead = lax.rem(here - pos + loops, loops)
        far_behind = lax.rem(pos - here + loops, loops)
        reach_ahead = jnp.where(core == 0, reach_even, reach_odd)
        reach_behind = jnp.where(core == 0, reach_odd, reach_even)
        by_ahead = far_ahead <= reach_ahead
        act(from_here & (j <= line) & (line + 1 < lines), 0)
        act(from_here & (j >= line) & (line > 0), 1)
        act(from_here | (by_ahead & (far_ahead < reach_ahead)), 2)
        act(from_here | (jnp.logical_not(by_ahead) & (far_behind < reach_behind)), 3)
        act(from_here | True, 4)

    def nearby(first, action):
        def step(t, _):
            far = (t + 1) // 2
            j = jnp.where(lax.rem(t, 2) == 1, line - far, line + far)

            @pl.when((j >= 0) & (j < lines))
            def _():
                action(j)
            return 0
        lax.fori_loop(first, 2 * lines - 1, step, 0)

    def own(k):
        own_pick(k).wait()
        for d in range(1, slabs):
            pick_copy(k, d).wait()
        rows = jnp.concatenate(
            [fetched[k, o].astype(jnp.float32) for o in range(slabs)], axis=0
        ).astype(jnp.bfloat16)
        mine = jnp.dot(choose, rows, preferred_element_type=jnp.float32)
        cand[k, me] = mine.astype(jnp.bfloat16)
        forward(k, line, here)

    def column(k):
        def action(j):
            arrive(k, j, here, core)
            forward(k, j, here)
        nearby(1, action)

    def ring(k, e):
        def action(j):
            behind_pos = lax.rem(here - e + loops, loops)
            ahead_pos = lax.rem(here + e, loops)
            reach_ahead = jnp.where(core == 0, reach_even, reach_odd)
            reach_behind = jnp.where(core == 0, reach_odd, reach_even)

            @pl.when(e <= reach_ahead)
            def _():
                arrive(k, j, behind_pos, core)
                forward(k, j, behind_pos)

            @pl.when(e <= reach_behind)
            def _():
                arrive(k, j, ahead_pos, core)
                forward(k, j, ahead_pos)
        nearby(0, action)

    def sibling(k):
        def step(t, _):
            arrive(k, t // loops, lax.rem(t, loops), 1 - core)
            return 0
        lax.fori_loop(0, lines * loops, step, 0)

    def multiply(k):
        docs_copy[k].wait()
        share_all = cand[k].reshape(units * share, chunk)

        def step(i, _):
            at = pl.ds(pl.multiple_of(i * tile, tile), tile)
            product = lax.dot_general(
                docs[k, at, :], share_all, (((1,), (1,)), ((), ())),
                preferred_element_type=jnp.float32,
            )
            if k == 0:
                acc[at, :] = product
            else:
                acc[at, :] += product
            return 0
        lax.fori_loop(0, n_docs // tile, step, 0)

    for k in range(min(2, chunks)):
        gather(k)
    own(0)
    column(0)
    for k in range(chunks):
        if k + 2 < chunks:
            gather(k + 2)
        ring(k, 1)
        if k + 1 < chunks:
            own(k + 1)
            column(k + 1)
        for e in range(2, half + 1):
            ring(k, e)
        if k > 0:
            sibling(k - 1)
            multiply(k - 1)
    sibling(chunks - 1)
    multiply(chunks - 1)

    cover_cols = jnp.transpose(cover_ref[...])
    weight_cols = jnp.transpose(weight_ref[...])
    total = jnp.zeros((1, units * share), jnp.float32)
    for j in range(n_docs // LANES):
        s = acc[j * LANES:(j + 1) * LANES, :] * scale
        gain = weight_cols[:, j:j + 1] * jnp.maximum(s - cover_cols[:, j:j + 1], 0.0)
        total = total + jnp.sum(gain, axis=0, keepdims=True)
    total = total / total_docs
    per_row = LANES // share
    for r in range(units // per_row):
        part[r] = total[:, r * LANES:(r + 1) * LANES]

    def term_copy(d):
        other = lax.rem(me + d, units)
        return pltpu.make_async_remote_copy(
            src_ref=part.at[other // per_row], dst_ref=terms.at[d],
            send_sem=term_send.at[d], recv_sem=term_recv.at[d],
            device_id=(other // loops, lax.rem(other, loops)), device_id_type=MESH,
        )

    def send_term(d, _):
        term_copy(d).start()
        return 0

    def take_term(d, _):
        term_copy(d).wait()
        return 0

    lax.fori_loop(1, units, send_term, 0)
    terms[0] = part[me // per_row]
    for k in range(chunks):
        def finish(t, _, k=k):
            forward(k, t // loops, lax.rem(t, loops), finish=True)
            return 0
        lax.fori_loop(0, lines * loops, finish, 0)
    lax.fori_loop(1, units, take_term, 0)
    out_ref[...] = jnp.sum(terms[...], axis=0)


def body(dims, doc_pool, cand_owner, cand_row, elements, coverage, elem_weight):
    slabs, loops, share, cap, chunks, chunk, tile, _, _ = dims
    pool_rows, width = doc_pool.shape[2:]
    n_docs = elements.shape[2]
    units = slabs * loops
    per_row = LANES // share
    vmem = pl.BlockSpec(memory_space=pltpu.VMEM)
    hbm = pl.BlockSpec(memory_space=pl.ANY)
    dma = pltpu.SemaphoreType.DMA
    out = pl.pallas_call(
        functools.partial(kernel, dims),
        out_shape=jax.ShapeDtypeStruct((1, LANES), jnp.float32),
        in_specs=[vmem, vmem, vmem, vmem, hbm, hbm],
        out_specs=vmem,
        scratch_shapes=[
            pltpu.VMEM((pool_rows, width), jnp.bfloat16),
            pltpu.VMEM((chunks, n_docs, chunk), jnp.bfloat16),
            pltpu.VMEM((slabs, SUB, LANES), jnp.int32),
            pltpu.VMEM((slabs, SUB, LANES), jnp.int32),
            pltpu.VMEM((chunks, slabs, cap, chunk), jnp.bfloat16),
            pltpu.VMEM((chunks, slabs, cap, chunk), jnp.bfloat16),
            pltpu.VMEM((chunks, units, share, chunk), jnp.bfloat16),
            pltpu.VMEM((n_docs, units * share), jnp.float32),
            pltpu.VMEM((units // per_row, 1, LANES), jnp.float32),
            pltpu.VMEM((units, 1, LANES), jnp.float32),
            dma((chunks,)),
            dma((chunks,)),
            dma((slabs,)),
            dma((slabs,)),
            dma((chunks, slabs)),
            dma((chunks, slabs)),
            dma((chunks + 1,)),
            dma((chunks, units // 2, 5)),
            dma((chunks, units)),
            dma((units,)),
            dma((units,)),
        ],
        compiler_params=pltpu.CompilerParams(
            collective_id=0, has_side_effects=True, vmem_limit_bytes=60 * 2**20
        ),
    )(
        cand_owner.reshape(1, share),
        cand_row.reshape(1, share),
        coverage.reshape(n_docs // LANES, LANES),
        elem_weight.reshape(n_docs // LANES, LANES),
        doc_pool.reshape(pool_rows, width),
        elements.reshape(n_docs, width),
    )
    me = lax.axis_index("slab") * loops + lax.axis_index("loop")
    mine = lax.dynamic_slice(out, (0, lax.rem(me, per_row) * share), (1, share))
    return mine.reshape(1, 1, share)


def solution(mesh):
    slabs, loops = mesh.shape["slab"], mesh.shape["loop"]

    def whole(doc_pool, cand_owner, cand_row, elements, coverage, elem_weight):
        share = cand_row.shape[2]
        width = doc_pool.shape[3]
        n_docs = elements.shape[2]
        cap = max(2, 2 * share // slabs)
        chunks = 4
        dims = (
            slabs, loops, share, cap, chunks, width // chunks, min(512, n_docs),
            float(n_docs * slabs * loops), float(width) ** (-0.5),
        )
        placed = (
            P("slab", "loop", None, None),
            P("slab", "loop", None, None),
            P("slab", "loop", None),
            P("slab", "loop", None, None),
            P("slab", "loop", None),
            P("slab", "loop", None),
        )
        return jax.shard_map(
            functools.partial(body, dims), mesh=mesh, in_specs=placed,
            out_specs=P("slab", "loop", None), check_vma=False,
        )(doc_pool, cand_owner, cand_row, elements, coverage, elem_weight)

    return whole
```

time: 159 us -> 87 us (0.55)
  Pallas kernels: 0 us -> 85.5 us
  waiting for transfers between devices: 69.7 us -> 0 us
  blocking collectives: 50.9 us -> 0 us
  matrix products: 14 us -> 0 us
  between operations: 13.5 us -> 0.01 us
  other arithmetic: 4.71 us -> 0 us
  starting transfers between devices: 3.45 us -> 0 us
    pallas_call x0 -> x1, Pallas kernels: none -> 85.5 us  [body(): pl.pallas_call(functools.partial(kernel, dims), out_shape=jax.ShapeDtypeS...]
    all_gather x1 -> x0, waiting for transfers between devices: 60.8 us -> none  [body(): lax.all_gather(cand_rows, ('slab', 'loop'), axis=0, tiled=True)]
    unnamed x1 -> x0, blocking collectives: 39.2 us -> none
    dot_general x1 -> x0, matrix products: 14 us -> none  [body(): lax.dot_general(docs, lax.all_gather(cand_rows, ('slab', 'loop'), axis=0,...]
    all_to_all x1 -> x0, blocking collectives: 11.7 us -> none  [body(): lax.all_to_all(requests, 'slab', split_axis=0, concat_axis=0, tiled=True)]
    all_to_all x1 -> x0, waiting for transfers between devices: 8.91 us -> none  [body(): lax.all_to_all(doc_rows, 'slab', split_axis=0, concat_axis=0, tiled=True)]
    all_to_all x1 -> x0, starting transfers between devices: 3.41 us -> none  [body(): lax.all_to_all(doc_rows, 'slab', split_axis=0, concat_axis=0, tiled=True)]
    select_n x4 -> x0, other arithmetic: 2.27 us -> none  [the longest x2 1.39 us: body(): jnp.take(fetched.reshape(slab_count * slot_cap, width), slot_id, axis=0)]
  transfers between devices with their start and end apart: 2 -> 0, of which waited for: 2 -> 0; matrix products, arithmetic and copies ran while one was open for 0% -> 0% of each run, Pallas kernels for 0% -> 0%
where the time goes in v1:
time: 87 us; the launch traced here: 86.8 us
  Pallas kernels  85.5 us (98%)
  local copies, waits for them, and re-layouts  1.27 us (1%)
    pallas_call x1, Pallas kernels, body(): pl.pallas_call(functools.partial(kernel, dims), out_shape=jax.ShapeDtypeS...  85.5 us

profile of v1, /device:TPU:0, one launch (start us, length us, event | category | flops | bytes accessed | tf_op | source)
XLA Modules:
  0.0 86.8 jit_solution(1848726821287849659)
XLA Ops:
  0.0 85.5 %shard_map.64 = f32[1,128]{1,0:T(1,128)} custom-call(s32[1,16]{1,0:T(1,128)} %bitcast.12, s32[1,16]{1,0:T(1,128)} %bitcast.13, f32[16,128]{1,0:T(8,128)} %bitcast.10, f32[16,128]{1,0:T(8,128)} %bitcast.11, bf16[256,4096]{1,0:T(8,128)(2,1)} %bitcast.9, bf16[2048,4096]{1,0:T(8,128)(2,1)} %bitcast.8), custom_call_target="tpu_custom_call" | custom-call | tf_op jit(solution)/shard_map/pallas_call | solution.py:338
  85.5 1.3 %dynamic-slice_bitcast_fusion = f32[1,1,16]{2,1,0:T(1,128)} fusion(f32[1,128]{1,0:T(1,128)} %shard_map.64, s32[]{:T(128)S(6)} %select_n.3), kind=kLoop, calls=%fused_computation | loop fusion | bytes 132 | tf_op jit(solution)/shard_map/reshape | solution.py:379

commit v2 on v1

--- a/solution.py
+++ b/solution.py
@@ -16,9 +16,10 @@
     dims,
     owner_ref, row_ref, cover_ref, weight_ref, pool_hbm, docs_hbm,
     out_ref,
-    pool, docs, req_out, req_in, picked, fetched, cand, acc, part, terms,
+    pool, docs, req_out, req_in, picked, fetched, cand, acc, part, slab_terms,
+    loop_terms,
     pool_sem, docs_sem, req_send, req_recv, pick_send, pick_recv, self_sem,
-    unit_send, unit_recv, term_send, term_recv,
+    unit_send, line_send, unit_recv, slab_send, slab_recv, loop_send, loop_recv,
 ):
     slabs, loops, share, cap, chunks, chunk, tile, total_docs, scale = dims
     lines = slabs // 2
@@ -31,6 +32,7 @@
     core = lax.rem(slab, 2)
     me = slab * loops + loop
     half = loops // 2
+    pieces = 2
 
     def loop_of(pos):
         return jnp.where(pos < half, 2 * pos, 2 * (loops - 1 - pos) + 1)
@@ -56,14 +58,13 @@
 
     barrier = pltpu.get_barrier_semaphore()
 
-    def greet(d, _):
-        other = lax.rem(me + d, units)
-        pl.semaphore_signal(
-            barrier, inc=1, device_id=(other // loops, lax.rem(other, loops)), device_id_type=MESH
-        )
-        return 0
-
-    lax.fori_loop(1, units, greet, 0)
+    def greet(device):
+        pl.semaphore_signal(barrier, inc=1, device_id=device, device_id_type=MESH)
+
+    for d in range(1, slabs):
+        greet((lax.rem(slab + d, slabs), loop))
+    for d in range(1, loops):
+        greet((slab, lax.rem(loop + d, loops)))
     for k in range(chunks):
         pool_copy[k].start()
     for k in range(chunks):
@@ -97,7 +98,7 @@
         1.0, 0.0,
     ).astype(jnp.bfloat16)
 
-    pl.semaphore_wait(barrier, units - 1)
+    pl.semaphore_wait(barrier, slabs + loops - 2)
 
     def req_copy(d):
         other = lax.rem(slab + d, slabs)
@@ -152,20 +153,18 @@
 
     def unit_copy(k, j, pos, way):
         u = unit_of(j, pos, core)
-        if way == 0:
-            device = (2 * jnp.minimum(line + 1, lines - 1) + core, loop)
-        elif way == 1:
-            device = (2 * jnp.maximum(line - 1, 0) + core, loop)
-        elif way == 2:
-            device = (slab, ahead)
-        elif way == 3:
-            device = (slab, behind)
-        else:
-            device = (2 * line + 1 - core, loop)
+        device = ((slab, ahead), (slab, behind), (2 * line + 1 - core, loop))[way]
         return pltpu.make_async_remote_copy(
             src_ref=cand.at[k, u], dst_ref=cand.at[k, u],
             send_sem=unit_send.at[k, j * loops + pos, way], recv_sem=unit_recv.at[k, u],
             device_id=device, device_id_type=MESH,
+        )
+
+    def line_copy(k, d):
+        return pltpu.make_async_remote_copy(
+            src_ref=cand.at[k, me], dst_ref=cand.at[k, me],
+            send_sem=line_send.at[k, d], recv_sem=unit_recv.at[k, me],
+            device_id=(lax.rem(slab + 2 * d, slabs), loop), device_id_type=MESH,
         )
 
     def arrive(k, j, pos, c):
@@ -193,11 +192,9 @@
         reach_ahead = jnp.where(core == 0, reach_even, reach_odd)
         reach_behind = jnp.where(core == 0, reach_odd, reach_even)
         by_ahead = far_ahead <= reach_ahead
-        act(from_here & (j <= line) & (line + 1 < lines), 0)
-        act(from_here & (j >= line) & (line > 0), 1)
-        act(from_here | (by_ahead & (far_ahead < reach_ahead)), 2)
-        act(from_here | (jnp.logical_not(by_ahead) & (far_behind < reach_behind)), 3)
-        act(from_here | True, 4)
+        act(from_here | (by_ahead & (far_ahead < reach_ahead)), 0)
+        act(from_here | (jnp.logical_not(by_ahead) & (far_behind < reach_behind)), 1)
+        act(from_here | True, 2)
 
     def nearby(first, action):
         def step(t, _):
@@ -220,6 +217,8 @@
         mine = jnp.dot(choose, rows, preferred_element_type=jnp.float32)
         cand[k, me] = mine.astype(jnp.bfloat16)
         forward(k, line, here)
+        for d in range(1, lines):
+            line_copy(k, d).start()
 
     def column(k):
         def action(j):
@@ -251,12 +250,13 @@
             return 0
         lax.fori_loop(0, lines * loops, step, 0)
 
-    def multiply(k):
-        docs_copy[k].wait()
+    def multiply(k, piece):
+        if piece == 0:
+            docs_copy[k].wait()
         share_all = cand[k].reshape(units * share, chunk)
-
-        def step(i, _):
-            at = pl.ds(pl.multiple_of(i * tile, tile), tile)
+        rows = n_docs // pieces
+        for i in range(rows // tile):
+            at = pl.ds(piece * rows + i * tile, tile)
             product = lax.dot_general(
                 docs[k, at, :], share_all, (((1,), (1,)), ((), ())),
                 preferred_element_type=jnp.float32,
@@ -265,27 +265,28 @@
                 acc[at, :] = product
             else:
                 acc[at, :] += product
-            return 0
-        lax.fori_loop(0, n_docs // tile, step, 0)
-
+
+    for k in range(chunks):
+        gather(k)
     for k in range(min(2, chunks)):
-        gather(k)
-    own(0)
-    column(0)
-    for k in range(chunks):
-        if k + 2 < chunks:
-            gather(k + 2)
-        ring(k, 1)
-        if k + 1 < chunks:
-            own(k + 1)
-            column(k + 1)
-        for e in range(2, half + 1):
-            ring(k, e)
-        if k > 0:
-            sibling(k - 1)
-            multiply(k - 1)
-    sibling(chunks - 1)
-    multiply(chunks - 1)
+        own(k)
+    for t in range(chunks + half + 1):
+        stages = []
+        if 0 < t < chunks - 1:
+            stages.append(functools.partial(own, t + 1))
+        if t < chunks:
+            stages.append(functools.partial(column, t))
+        for e in range(1, half + 1):
+            if 0 <= t - e < chunks:
+                stages.append(functools.partial(ring, t - e, e))
+        if 0 <= t - half < chunks:
+            stages.append(functools.partial(sibling, t - half))
+        done = t - half - 1
+        for piece in range(max(pieces, len(stages))):
+            if piece < len(stages):
+                stages[piece]()
+            if done >= 0 and piece < pieces:
+                multiply(done, piece)
 
     cover_cols = jnp.transpose(cover_ref[...])
     weight_cols = jnp.transpose(weight_ref[...])
@@ -295,35 +296,44 @@
         gain = weight_cols[:, j:j + 1] * jnp.maximum(s - cover_cols[:, j:j + 1], 0.0)
         total = total + jnp.sum(gain, axis=0, keepdims=True)
     total = total / total_docs
-    per_row = LANES // share
-    for r in range(units // per_row):
+    for r in range(units * share // LANES):
         part[r] = total[:, r * LANES:(r + 1) * LANES]
-
-    def term_copy(d):
-        other = lax.rem(me + d, units)
-        return pltpu.make_async_remote_copy(
-            src_ref=part.at[other // per_row], dst_ref=terms.at[d],
-            send_sem=term_send.at[d], recv_sem=term_recv.at[d],
-            device_id=(other // loops, lax.rem(other, loops)), device_id_type=MESH,
-        )
-
-    def send_term(d, _):
-        term_copy(d).start()
-        return 0
-
-    def take_term(d, _):
-        term_copy(d).wait()
-        return 0
-
-    lax.fori_loop(1, units, send_term, 0)
-    terms[0] = part[me // per_row]
+    per_row = LANES // (loops * share)
+
+    def slab_term(d):
+        other = lax.rem(slab + d, slabs)
+        return pltpu.make_async_remote_copy(
+            src_ref=part.at[other // per_row], dst_ref=slab_terms.at[d],
+            send_sem=slab_send.at[d], recv_sem=slab_recv.at[d],
+            device_id=(other, loop), device_id_type=MESH,
+        )
+
+    def loop_term(d):
+        return pltpu.make_async_remote_copy(
+            src_ref=loop_terms.at[0], dst_ref=loop_terms.at[d],
+            send_sem=loop_send.at[d], recv_sem=loop_recv.at[d],
+            device_id=(slab, lax.rem(loop + d, loops)), device_id_type=MESH,
+        )
+
+    for d in range(1, slabs):
+        slab_term(d).start()
+    slab_terms[0] = part[slab // per_row]
     for k in range(chunks):
+        for d in range(1, lines):
+            line_copy(k, d).wait_send()
+
         def finish(t, _, k=k):
             forward(k, t // loops, lax.rem(t, loops), finish=True)
             return 0
         lax.fori_loop(0, lines * loops, finish, 0)
-    lax.fori_loop(1, units, take_term, 0)
-    out_ref[...] = jnp.sum(terms[...], axis=0)
+    for d in range(1, slabs):
+        slab_term(d).wait()
+    loop_terms[0] = jnp.sum(slab_terms[...], axis=0)
+    for d in range(1, loops):
+        loop_term(d).start()
+    for d in range(1, loops):
+        loop_term(d).wait()
+    out_ref[...] = jnp.sum(loop_terms[...], axis=0)
 
 
 def body(dims, doc_pool, cand_owner, cand_row, elements, coverage, elem_weight):
@@ -349,8 +359,9 @@
             pltpu.VMEM((chunks, slabs, cap, chunk), jnp.bfloat16),
             pltpu.VMEM((chunks, units, share, chunk), jnp.bfloat16),
             pltpu.VMEM((n_docs, units * share), jnp.float32),
-            pltpu.VMEM((units // per_row, 1, LANES), jnp.float32),
-            pltpu.VMEM((units, 1, LANES), jnp.float32),
+            pltpu.VMEM((units * share // LANES, 1, LANES), jnp.float32),
+            pltpu.VMEM((slabs, 1, LANES), jnp.float32),
+            pltpu.VMEM((loops, 1, LANES), jnp.float32),
             dma((chunks,)),
             dma((chunks,)),
             dma((slabs,)),
@@ -358,10 +369,13 @@
             dma((chunks, slabs)),
             dma((chunks, slabs)),
             dma((chunks + 1,)),
-            dma((chunks, units // 2, 5)),
+            dma((chunks, units // 2, 3)),
+            dma((chunks, slabs // 2)),
             dma((chunks, units)),
-            dma((units,)),
-            dma((units,)),
+            dma((slabs,)),
+            dma((slabs,)),
+            dma((loops,)),
+            dma((loops,)),
         ],
         compiler_params=pltpu.CompilerParams(
             collective_id=0, has_side_effects=True, vmem_limit_bytes=60 * 2**20
@@ -389,7 +403,7 @@
         cap = max(2, 2 * share // slabs)
         chunks = 4
         dims = (
-            slabs, loops, share, cap, chunks, width // chunks, min(512, n_docs),
+            slabs, loops, share, cap, chunks, width // chunks, min(1024, n_docs),
             float(n_docs * slabs * loops), float(width) ** (-0.5),
         )
         placed = (

time: 87 us -> 58.7 us (0.67)
  Pallas kernels: 85.5 us -> 57.3 us
    pallas_call x1, Pallas kernels: 85.5 us -> 57.3 us  [body(): pl.pallas_call(functools.partial(kernel, dims), out_shape=jax.ShapeDtypeS...]
where the time goes in v2:
time: 58.7 us; the launch traced here: 58.5 us
  Pallas kernels  57.3 us (98%)
  local copies, waits for them, and re-layouts  1.27 us (2%)
    pallas_call x1, Pallas kernels, body(): pl.pallas_call(functools.partial(kernel, dims), out_shape=jax.ShapeDtypeS...  57.3 us
    reshape x1, local copies, waits for them, and re-layouts, body(): return mine.reshape(1, 1, share)  1.27 us

profile of v2, /device:TPU:0, one launch (start us, length us, event | category | flops | bytes accessed | tf_op | source)
XLA Modules:
  0.0 58.5 jit_solution(18124052448442050746)
XLA Ops:
  0.0 57.3 %shard_map.64 = f32[1,128]{1,0:T(1,128)} custom-call(s32[1,16]{1,0:T(1,128)} %bitcast.12, s32[1,16]{1,0:T(1,128)} %bitcast.13, f32[16,128]{1,0:T(8,128)} %bitcast.10, f32[16,128]{1,0:T(8,128)} %bitcast.11, bf16[256,4096]{1,0:T(8,128)(2,1)} %bitcast.9, bf16[2048,4096]{1,0:T(8,128)(2,1)} %bitcast.8), custom_call_target="tpu_custom_call" | custom-call | tf_op jit(solution)/shard_map/pallas_call | solution.py:348
  57.3 1.3 %dynamic-slice_bitcast_fusion = f32[1,1,16]{2,1,0:T(1,128)} fusion(f32[1,128]{1,0:T(1,128)} %shard_map.64, s32[]{:T(128)S(6)} %select_n.3), kind=kLoop, calls=%fused_computation | loop fusion | bytes 132 | tf_op jit(solution)/shard_map/reshape | solution.py:393

commit v3 on v2

--- a/solution.py
+++ b/solution.py
@@ -32,7 +32,7 @@
     core = lax.rem(slab, 2)
     me = slab * loops + loop
     half = loops // 2
-    pieces = 2
+    pieces = 4
 
     def loop_of(pos):
         return jnp.where(pos < half, 2 * pos, 2 * (loops - 1 - pos) + 1)
@@ -333,7 +333,15 @@
         loop_term(d).start()
     for d in range(1, loops):
         loop_term(d).wait()
-    out_ref[...] = jnp.sum(loop_terms[...], axis=0)
+    row = jnp.sum(loop_terms[...], axis=0)
+    first = lax.rem(slab, per_row) * loops * share + loop * share
+    mine = lax.broadcasted_iota(jnp.int32, (LANES, LANES), 0)
+    to = lax.broadcasted_iota(jnp.int32, (LANES, LANES), 1)
+    column_of = jnp.sum(
+        jnp.where(mine == to, jnp.broadcast_to(row, (LANES, LANES)), 0.0), axis=1, keepdims=True
+    )
+    moved = jnp.sum(jnp.where(mine == to + first, column_of, 0.0), axis=0, keepdims=True)
+    out_ref[...] = moved[:, :share]
 
 
 def body(dims, doc_pool, cand_owner, cand_row, elements, coverage, elem_weight):
@@ -341,13 +349,12 @@
     pool_rows, width = doc_pool.shape[2:]
     n_docs = elements.shape[2]
     units = slabs * loops
-    per_row = LANES // share
     vmem = pl.BlockSpec(memory_space=pltpu.VMEM)
     hbm = pl.BlockSpec(memory_space=pl.ANY)
     dma = pltpu.SemaphoreType.DMA
     out = pl.pallas_call(
         functools.partial(kernel, dims),
-        out_shape=jax.ShapeDtypeStruct((1, LANES), jnp.float32),
+        out_shape=jax.ShapeDtypeStruct((1, share), jnp.float32),
         in_specs=[vmem, vmem, vmem, vmem, hbm, hbm],
         out_specs=vmem,
         scratch_shapes=[
@@ -388,9 +395,7 @@
         doc_pool.reshape(pool_rows, width),
         elements.reshape(n_docs, width),
     )
-    me = lax.axis_index("slab") * loops + lax.axis_index("loop")
-    mine = lax.dynamic_slice(out, (0, lax.rem(me, per_row) * share), (1, share))
-    return mine.reshape(1, 1, share)
+    return out.reshape(1, 1, share)
 
 
 def solution(mesh):
@@ -403,7 +408,7 @@
         cap = max(2, 2 * share // slabs)
         chunks = 4
         dims = (
-            slabs, loops, share, cap, chunks, width // chunks, min(1024, n_docs),
+            slabs, loops, share, cap, chunks, width // chunks, min(512, n_docs),
             float(n_docs * slabs * loops), float(width) ** (-0.5),
         )
         placed = (

time: 58.7 us -> 58.4 us (level)
    reshape x1 -> x0, local copies, waits for them, and re-layouts: 1.27 us -> none  [body(): return mine.reshape(1, 1, share)]
    unnamed x0 -> x1, local copies, waits for them, and re-layouts: none -> 1.19 us
where the time goes in v3:
time: 58.4 us; the launch traced here: 58.2 us
  Pallas kernels  57 us (98%)
  local copies, waits for them, and re-layouts  1.19 us (2%)
    pallas_call x1, Pallas kernels, body(): pl.pallas_call(functools.partial(kernel, dims), out_shape=jax.ShapeDtypeS...  57 us
    unnamed x1, local copies, waits for them, and re-layouts  1.19 us

profile of v3, /device:TPU:0, one launch (start us, length us, event | category | flops | bytes accessed | tf_op | source)
XLA Modules:
  0.0 58.2 jit_solution(9577699340063717886)
XLA Ops:
  0.0 57.0 %shard_map.64 = f32[1,16]{1,0:T(1,128)} custom-call(s32[1,16]{1,0:T(1,128)} %bitcast.11, s32[1,16]{1,0:T(1,128)} %bitcast.12, f32[16,128]{1,0:T(8,128)} %bitcast.9, f32[16,128]{1,0:T(8,128)} %bitcast.10, bf16[256,4096]{1,0:T(8,128)(2,1)} %bitcast.8, bf16[2048,4096]{1,0:T(8,128)(2,1)} %bitcast.7), custom_call_target="tpu_custom_call" | custom-call | tf_op jit(solution)/shard_map/pallas_call | solution.py:355
  57.0 1.2 %copy.8 = f32[1,1,16]{2,1,0:T(1,128)} copy(f32[1,1,16]{2,1,0:T(1,128)} %bitcast.13) | data formatting | bytes 128
